TPU v7x, 256 devices: a whole 4x4x8 slice. The times are simulated.
256 devices in a mesh: grp: 32 (over y, x, core), mem: 8 (over z).
Axes of the slice: x: 4, y: 4, z: 8, core: 2. Of those that a mesh axis runs over, the one named last changes fastest.
Arguments:
- features: bfloat16 [131072, 512], P(('grp', 'mem')), may hold values from -6 to 6
- weight: bfloat16 [512, 512], replicated, may hold values from -0.25 to 0.25
- adj_tiles: bfloat16 [1024, 32, 128, 128], P(('grp', 'mem')), may hold values from -0.09375 to 0.09375
- adj_cols: int32 [1024, 32], P(('grp', 'mem')), may hold values from 0 to 31
- send_blocks: int32 [256, 32, 2], P(('grp', 'mem')), may hold values from -1 to 3, as said below
- read_tiles: bfloat16 [256, 32, 2, 128, 128], P(('grp', 'mem')), may hold values from -0.1875 to 0.1875
- read_rows: int32 [256, 32, 2], P(('grp', 'mem')), may hold values from 0 to 3
Outputs:
- output: bfloat16 [131072, 512], P(('grp', 'mem'))
Inputs may be any that keep to these rules, and one draw needn't show every extreme that they name: `send_blocks`: -1 marks an empty slot; the used slots of each entry come first. In every draw, for each m some group receives 2 blocks from every vertex block s * 8 + m.
All inputs are finite; a program needn't handle non-finite values.
Results may differ from a plain program's by a relative error of at most 0.0058.
Values may be sent and summed in bfloat16 or wider, within the bound.
No kernel may reach another device: no remote copies, remote signals or barrier semaphores. Data moves between devices by JAX's collectives and lax.ppermute only.
A program may use at most 128 MiB of HBM per device.

v0:
```python
import jax
import jax.numpy as jnp
from jax import lax
from jax.sharding import PartitionSpec as P


def per_device(features, weight, adj_tiles, adj_cols, send_blocks, read_tiles, read_rows):
    rows_here = features.shape[0]
    width = features.shape[1]
    tile_rows = adj_tiles.shape[2]
    block_count = rows_here // tile_rows
    group_rows = lax.all_gather(features, "mem", axis=0, tiled=True)
    group_tiles = group_rows.reshape(-1, tile_rows, width)
    chosen = jnp.take(group_tiles, adj_cols, axis=0)
    propagated = jnp.einsum("rkij,rkjf->rif", adj_tiles, chosen, preferred_element_type=jnp.float32)
    propagated = propagated.astype(jnp.bfloat16).reshape(rows_here, width)
    hidden = jnp.maximum(
        jnp.dot(propagated, weight, preferred_element_type=jnp.float32), 0.0
    ).astype(jnp.bfloat16)
    slot_lists = send_blocks[0]
    tiles_in = read_tiles[0]
    onehot = (
        read_rows[0][:, :, None] == jnp.arange(block_count, dtype=jnp.int32)[None, None, :]
    ).astype(jnp.float32)
    wanted = lax.all_to_all(slot_lists, "grp", split_axis=0, concat_axis=0, tiled=True)
    shard_rows = lax.all_gather(hidden, "grp", axis=0, tiled=True)
    group_count = shard_rows.shape[0] // rows_here
    pieces = shard_rows.reshape(group_count, block_count, tile_rows, width)
    safe_lists = jnp.clip(wanted, 0, block_count - 1)
    picked = pieces[jnp.arange(group_count, dtype=jnp.int32)[:, None], safe_lists]
    picked = jnp.where((wanted >= 0)[:, :, None, None], picked, jnp.zeros((), jnp.bfloat16))
    products = jnp.einsum("gkij,gkjf->gkif", tiles_in, picked, preferred_element_type=jnp.float32)
    aggregate = jnp.einsum("gkr,gkif->rif", onehot, products, precision=lax.Precision.HIGHEST)
    combined = hidden.astype(jnp.float32) + aggregate.reshape(rows_here, width)
    return combined.astype(jnp.bfloat16)


def solution(mesh):
    placed = (
        P(("grp", "mem"), None),
        P(),
        P(("grp", "mem"), None, None, None),
        P(("grp", "mem"), None),
        P(("grp", "mem"), None, None),
        P(("grp", "mem"), None, None, None, None),
        P(("grp", "mem"), None, None),
    )
    return jax.shard_map(
        per_device, mesh=mesh, in_specs=placed, out_specs=P(("grp", "mem"), None), check_vma=False
    )
```

profile of v0, /device:TPU:1, one launch (start us, length us, event | category | flops | bytes accessed | tf_op | source)
XLA Modules:
  0.0 239.2 jit_solution(8391985096716967767)
XLA Ops:
  6.5 0.0 copy-start
  6.5 0.0 all-gather.3.cloned.1.call-start
  6.5 0.7 all-gather.3.cloned.1.call-update
  7.3 0.0 all-gather.5.cloned.1.call-start
  7.3 0.7 compare_select_fusion
  8.0 0.1 reshape.58
  8.1 0.7 compare_and_fusion
  8.8 58.8 %all-gather.3.cloned.1.call-done = bf16[4096,512]{1,0:T(8,128)(2,1)} async-done(((bf16[512,512]{1,0:T(8,128)(2,1)}), bf16[4096,512]{1,0:T(8,128)(2,1)}) %all-gather.3.cloned.1.call-update) | async-done | bytes 4194320 | tf_op jit(solution)/shard_map/all_gather | solution.py:12
  67.5 10.5 %gather_fusion = bf16[128,128,512]{2,1,0:T(8,128)(2,1)} fusion(bf16[32,128,512]{2,1,0:T(8,128)(2,1)} %bitcast.39, s32[1024]{0:T(1024)S(1)} %pad_clamp_fusion), kind=kCustom, calls=%fused_computation | custom fusion | bytes 33554944 | tf_op jit(solution)/shard_map/jit(_take)/gather | solution.py:14
  78.0 0.0 copy-start.4
  78.0 10.4 %fusion.11 = bf16[4,512,128]{1,2,0:T(8,128)(2,1)S(1)} fusion(bf16[4,32,128,128]{3,2,1,0:T(8,128)(2,1)} %param.9, bf16[4,32,128,512]{3,2,1,0:T(8,128)(2,1)} %bitcast.41, pred[4,32]{1,0:T(4,128)(4,1)S(1)} %compare_and_fusion), kind=kOutput, calls=%fused_computation.14 | convolution fusion | flops 2156134400 | bytes 21495936 | tf_op jit(solution)/shard_map/rkij,rkjf->rif/dot_general | solution.py:15
  88.4 0.0 copy-done.4
  88.4 1.2 fusion.14
  89.7 0.0 all-gather.5.cloned.1.call-update
  89.7 0.0 copy-done.3
  89.7 0.1 copy.22
  89.8 14.5 %all_to_all.9 = s32[32,1,2]{2,1,0:T(1,128)S(1)} all-to-all(s32[32,1,2]{2,1,0:T(1,128)S(1)} %copy.22), channel_id=1, replica_groups=mesh['grp'=32,'mem'=8] {'grp'}, dimensions={0} | all-to-all | bytes 512 | tf_op jit(solution)/shard_map/all_to_all | solution.py:25
  104.3 0.1 copy.23
  104.4 0.1 copy.24
  104.5 0.1 copy.26
  104.6 0.1 reshape.64
  104.7 61.9 %all-gather.5.cloned.1.call-done = bf16[16384,512]{1,0:T(8,128)(2,1)} async-done(((bf16[512,512]{1,0:T(8,128)(2,1)}), bf16[16384,512]{1,0:T(8,128)(2,1)}) %all-gather.5.cloned.1.call-update) | async-done | bytes 16777232 | tf_op jit(solution)/shard_map/all_gather | solution.py:26
  166.6 11.6 %gather_fusion.1 = bf16[64,128,512]{2,1,0:T(8,128)(2,1)} fusion(bf16[32,4,128,512]{3,2,1,0:T(8,128)(2,1)} %bitcast.42, s32[64]{0:T(128)S(1)} %reshape.64), kind=kCustom, calls=%fused_computation.1 | custom fusion | bytes 16777728 | tf_op jit(solution)/shard_map/gather | solution.py:30
  178.2 11.9 %copy.27 = bf16[64,128,512]{1,2,0:T(8,128)(2,1)} copy(bf16[64,128,512]{2,1,0:T(8,128)(2,1)} %gather_fusion.1) | data formatting | bytes 16777216 | tf_op jit(solution)/shard_map/gather | solution.py:30
  190.1 0.0 copy-done
  190.1 11.5 %convolution_bitcast_fusion = f32[32,2,128,512]{2,3,1,0:T(8,128)} fusion(bf16[32,2,128,512]{2,3,1,0:T(8,128)(2,1)} %bitcast.40, pred[32,2]{1,0:T(8,128)(4,1)S(1)} %copy.24, bf16[1,32,2,128,128]{4,3,2,1,0:T(8,128)(2,1)S(1)} %copy-done), kind=kOutput, calls=%fused_computation.5 | convolution fusion | flops 1077936128 | bytes 27263040 | tf_op jit(solution)/shard_map/gkij,gkjf->gkif/dot_general | solution.py:32
  201.6 20.0 %copy.28 = f32[32,2,128,512]{3,0,1,2:T(8,128)} copy(f32[32,2,128,512]{2,3,1,0:T(8,128)} %convolution_bitcast_fusion) | data formatting | bytes 33554432 | tf_op jit(solution)/shard_map/gkij,gkjf->gkif/dot_general | solution.py:32
  221.6 0.0 copy-done.2
  221.6 9.4 %convolution_bitcast_fusion.1 = f32[4,128,512]{2,0,1:T(4,128)S(1)} fusion(f32[32,2,128,512]{3,0,1,2:T(8,128)} %copy.28, s32[32,2]{0,1:T(2,128)S(1)} %bitcast.43), kind=kOutput, calls=%fused_computation.11 | convolution fusion | flops 201326848 | bytes 17826048 | tf_op jit(solution)/shard_map/gkr,gkif->rif/dot_general | solution.py:33
  231.0 0.3 copy.29
  231.4 0.0 copy-done.1
  231.4 1.0 fusion.15
  (6 shorter events, 0.0 us)
Async XLA Ops:
  6.5 183.6 %copy-start = (bf16[1,32,2,128,128]{4,3,2,1,0:T(8,128)(2,1)S(1)}, bf16[1,32,2,128,128]{4,3,2,1,0:T(8,128)(2,1)}, u32[]{:S(2)}) copy-start(bf16[1,32,2,128,128]{4,3,2,1,0:T(8,128)(2,1)} %param.12) | copy-start | bytes 6291460
  6.5 61.0 %all-gather.3.cloned.1.call-start = ((), (), s32[]{:S(2)}) async-start(), calls=%async_computation.1 | async-start | bytes 4718592 | tf_op jit(solution)/shard_map/all_gather | solution.py:12
  7.3 159.3 %all-gather.5.cloned.1.call-start = ((), (), s32[]{:S(2)}) async-start(), calls=%async_computation.2 | async-start | bytes 17301504 | tf_op jit(solution)/shard_map/all_gather | solution.py:26
  78.0 10.4 %copy-start.4 = (bf16[512,512]{1,0:T(8,128)(2,1)S(1)}, bf16[512,512]{1,0:T(8,128)(2,1)}, u32[]{:S(2)}) copy-start(bf16[512,512]{1,0:T(8,128)(2,1)} %param.8) | copy-start | bytes 1572868
  78.0 11.7 %copy-start.3 = (s32[1,32,2]{1,2,0:T(2,128)S(1)}, s32[1,32,2]{1,2,0:T(2,128)}, u32[]{:S(2)}) copy-start(s32[1,32,2]{1,2,0:T(2,128)} %param.11) | copy-start | bytes 772
  201.6 20.0 %copy-start.2 = (s32[1,32,2]{1,2,0:T(2,128)S(1)}, s32[1,32,2]{1,2,0:T(2,128)}, u32[]{:S(2)}) copy-start(s32[1,32,2]{1,2,0:T(2,128)} %param.13) | copy-start | bytes 772
  221.6 9.8 %copy-start.1 = (bf16[512,512]{1,0:T(8,128)(2,1)S(1)}, bf16[512,512]{1,0:T(8,128)(2,1)}, u32[]{:S(2)}) copy-start(bf16[512,512]{1,0:T(8,128)(2,1)} %fusion.14) | copy-start | bytes 1572868
Sparse Core Ops, SparseCore 0:
  9.1 58.3 all-gather.2
  89.8 76.7 all-gather.4
where the time goes:
time: 240 us; the launch traced here: 239 us
  waiting for transfers between devices  121 us (50%)
  local copies, waits for them, and re-layouts  54.9 us (23%)
  matrix products  32.5 us (14%)
  blocking collectives  14.5 us (6%)
  between operations  13.5 us (6%)
    all_gather x1, waiting for transfers between devices, per_device(): shard_rows = lax.all_gather(hidden, 'grp', axis=0, tiled=True)  61.9 us
    all_gather x1, waiting for transfers between devices, per_device(): group_rows = lax.all_gather(features, 'mem', axis=0, tiled=True)  58.8 us
    gather x2, local copies, waits for them, and re-layouts, per_device(): pieces[jnp.arange(group_count, dtype=jnp.int32)[:, None], safe_lists]  23.5 us
    dot_general x1, local copies, waits for them, and re-layouts, per_device(): jnp.einsum('gkij,gkjf->gkif', tiles_in, picked, preferred_element_type=jn...  20 us
    all_to_all x1, blocking collectives, per_device(): lax.all_to_all(slot_lists, 'grp', split_axis=0, concat_axis=0, tiled=True)  14.5 us
    dot_general x1, matrix products, per_device(): jnp.einsum('gkij,gkjf->gkif', tiles_in, picked, preferred_element_type=jn...  11.5 us
    gather x1, local copies, waits for them, and re-layouts, per_device(): chosen = jnp.take(group_tiles, adj_cols, axis=0)  10.5 us
    dot_general x1, matrix products, per_device(): jnp.einsum('rkij,rkjf->rif', adj_tiles, chosen, preferred_element_type=jn...  10.4 us
  transfers between devices with their start and end apart: 2, of which 2 were waited for; matrix products, arithmetic and copies ran while one was open for 1% of the time, Pallas kernels for 0%

commit v1 on v0

--- a/solution.py
+++ b/solution.py
@@ -23,7 +23,10 @@
         read_rows[0][:, :, None] == jnp.arange(block_count, dtype=jnp.int32)[None, None, :]
     ).astype(jnp.float32)
     wanted = lax.all_to_all(slot_lists, "grp", split_axis=0, concat_axis=0, tiled=True)
-    shard_rows = lax.all_gather(hidden, "grp", axis=0, tiled=True)
+    shard_rows = jnp.concatenate(
+        lax.all_to_all(jnp.stack([hidden for _ in range(lax.axis_size("grp"))]), "grp", 0, 0),
+        axis=0,
+    )
     group_count = shard_rows.shape[0] // rows_here
     pieces = shard_rows.reshape(group_count, block_count, tile_rows, width)
     safe_lists = jnp.clip(wanted, 0, block_count - 1)

time: 240 us -> 387 us (1.61)
  the two profiles are of different devices: /device:TPU:1 before, /device:TPU:96 now
where the time goes in v1:
time: 387 us; the launch traced here: 386 us
  waiting for transfers between devices  261 us (67%)
  local copies, waits for them, and re-layouts  62.1 us (16%)
  matrix products  31.7 us (8%)
  starting transfers between devices  14.7 us (4%)
  between operations  13.5 us (3%)
    all_to_all x1, waiting for transfers between devices, per_device(): lax.all_to_all(jnp.stack([hidden for _ in range(lax.axis_size('grp'))]),...  213 us
    all_gather x1, waiting for transfers between devices, per_device(): group_rows = lax.all_gather(features, 'mem', axis=0, tiled=True)  47.8 us
    gather x2, local copies, waits for them, and re-layouts, per_device(): pieces[jnp.arange(group_count, dtype=jnp.int32)[:, None], safe_lists]  23.5 us
    dot_general x1, local copies, waits for them, and re-layouts, per_device(): jnp.einsum('gkij,gkjf->gkif', tiles_in, picked, preferred_element_type=jn...  20 us
    dot_general x1, matrix products, per_device(): jnp.einsum('gkij,gkjf->gkif', tiles_in, picked, preferred_element_type=jn...  11.5 us
    gather x1, local copies, waits for them, and re-layouts, per_device(): chosen = jnp.take(group_tiles, adj_cols, axis=0)  10.5 us
    dot_general x1, matrix products, per_device(): jnp.einsum('rkij,rkjf->rif', adj_tiles, chosen, preferred_element_type=jn...  10.4 us
    dot_general x1, matrix products, per_device(): jnp.einsum('gkr,gkif->rif', onehot, products, precision=lax.Precision.HIG...  9.34 us
  transfers between devices with their start and end apart: 3, of which 2 were waited for; matrix products, arithmetic and copies ran while one was open for 6% of the time, Pallas kernels for 0%

profile of v1, /device:TPU:96, one launch (start us, length us, event | category | flops | bytes accessed | tf_op | source)
XLA Modules:
  0.0 385.5 jit_solution(12342572484486253613)
XLA Ops:
  6.5 0.0 copy-start
  6.5 0.0 all-gather.2.cloned.1.call-start
  6.5 0.7 all-gather.2.cloned.1.call-update
  7.3 1.4 copy.29
  8.6 7.3 %all-to-all-start = ((s32[32,1,2]{2,1,0:T(1,128)}), s32[32,1,2]{2,1,0:T(1,128)S(1)}, u32[]{:S(2)}, u32[]{:S(2)}) async-start(s32[32,1,2]{2,1,0:T(1,128)} %copy.29), calls=%async_computation | async-start | bytes 32768 | tf_op jit(solution)/shard_map/all_to_all | solution.py:25
  15.9 0.7 compare_select_fusion
  16.6 0.1 reshape.56
  16.7 0.7 compare_and_fusion
  17.4 47.8 %all-gather.2.cloned.1.call-done = bf16[4096,512]{1,0:T(8,128)(2,1)} async-done(((bf16[512,512]{1,0:T(8,128)(2,1)}), bf16[4096,512]{1,0:T(8,128)(2,1)}) %all-gather.2.cloned.1.call-update) | async-done | bytes 4194320 | tf_op jit(solution)/shard_map/all_gather | solution.py:12
  65.2 10.5 %gather_fusion = bf16[128,128,512]{2,1,0:T(8,128)(2,1)} fusion(bf16[32,128,512]{2,1,0:T(8,128)(2,1)} %bitcast.39, s32[1024]{0:T(1024)S(1)} %pad_clamp_fusion), kind=kCustom, calls=%fused_computation | custom fusion | bytes 33554944 | tf_op jit(solution)/shard_map/jit(_take)/gather | solution.py:14
  75.7 0.0 copy-start.2
  75.7 10.4 %fusion.11 = bf16[4,512,128]{1,2,0:T(8,128)(2,1)S(1)} fusion(bf16[4,32,128,128]{3,2,1,0:T(8,128)(2,1)} %param.9, bf16[4,32,128,512]{3,2,1,0:T(8,128)(2,1)} %bitcast.41, pred[4,32]{1,0:T(4,128)(4,1)S(1)} %compare_and_fusion), kind=kOutput, calls=%fused_computation.14 | convolution fusion | flops 2156134400 | bytes 21495936 | tf_op jit(solution)/shard_map/rkij,rkjf->rif/dot_general | solution.py:15
  86.1 0.0 copy-done.2
  86.1 0.4 fusion.14
  86.5 0.0 all-to-all-done
  86.6 5.9 %stack.2 = bf16[32,512,512]{2,1,0:T(8,128)(2,1)} broadcast(bf16[512,512]{1,0:T(8,128)(2,1)S(1)} %fusion.14), dimensions={1,2} | broadcast | bytes 17301504 | tf_op jit(solution)/shard_map/stack | solution.py:27
  92.5 7.4 %all-to-all-start.1 = ((bf16[32,512,512]{2,1,0:T(8,128)(2,1)}), bf16[32,512,512]{2,1,0:T(8,128)(2,1)}, u32[]{:S(2)}, u32[]{:S(2)}) async-start(bf16[32,512,512]{2,1,0:T(8,128)(2,1)} %stack.2), calls=%async_computation.1 | async-start | bytes 33554432 | tf_op jit(solution)/shard_map/all_to_all | solution.py:27
  99.9 0.1 copy.30
  100.0 0.1 copy.33
  100.1 0.1 reshape.62
  100.2 0.1 copy.31
  100.3 212.7 %all-to-all-done.1 = bf16[32,512,512]{2,1,0:T(8,128)(2,1)} async-done(((bf16[32,512,512]{2,1,0:T(8,128)(2,1)}), bf16[32,512,512]{2,1,0:T(8,128)(2,1)}, u32[]{:S(2)}, u32[]{:S(2)}) %all-to-all-start.1) | async-done | bytes 16777248 | tf_op jit(solution)/shard_map/all_to_all | solution.py:27
  313.0 11.6 %gather_fusion.1 = bf16[64,128,512]{2,1,0:T(8,128)(2,1)} fusion(bf16[32,4,128,512]{3,2,1,0:T(8,128)(2,1)} %bitcast.10, s32[64]{0:T(128)S(1)} %reshape.62), kind=kCustom, calls=%fused_computation.1 | custom fusion | bytes 16777728 | tf_op jit(solution)/shard_map/gather | solution.py:33
  324.6 11.9 %copy.34 = bf16[32,2,128,512]{2,3,1,0:T(8,128)(2,1)} copy(bf16[32,2,128,512]{3,2,1,0:T(8,128)(2,1)} %bitcast.40) | data formatting | bytes 16777216 | tf_op jit(solution)/shard_map/gather | solution.py:33
  336.5 0.0 copy-done
  336.5 11.5 %convolution_bitcast_fusion = f32[32,2,128,512]{2,3,1,0:T(8,128)} fusion(bf16[32,2,128,512]{2,3,1,0:T(8,128)(2,1)} %copy.34, pred[32,2]{1,0:T(8,128)(4,1)S(1)} %copy.31, bf16[1,32,2,128,128]{4,3,2,1,0:T(8,128)(2,1)S(1)} %copy-done), kind=kOutput, calls=%fused_computation.5 | convolution fusion | flops 1077936128 | bytes 27263040 | tf_op jit(solution)/shard_map/gkij,gkjf->gkif/dot_general | solution.py:35
  348.0 0.0 copy-start.1
  348.0 20.0 %copy.35 = f32[32,2,128,512]{3,0,1,2:T(8,128)} copy(f32[32,2,128,512]{2,3,1,0:T(8,128)} %convolution_bitcast_fusion) | data formatting | bytes 33554432 | tf_op jit(solution)/shard_map/gkij,gkjf->gkif/dot_general | solution.py:35
  368.0 0.0 copy-done.1
  368.0 9.3 %convolution_bitcast_fusion.1 = f32[4,128,512]{2,0,1:T(4,128)S(1)} fusion(f32[32,2,128,512]{3,0,1,2:T(8,128)} %copy.35, s32[32,2]{0,1:T(2,128)S(1)} %bitcast.42), kind=kOutput, calls=%fused_computation.11 | convolution fusion | flops 201326848 | bytes 17826048 | tf_op jit(solution)/shard_map/gkr,gkif->rif/dot_general | solution.py:36
  377.3 0.3 copy.36
  377.7 1.0 fusion.15
  (3 shorter events, 0.0 us)
Async XLA Ops:
  6.5 329.9 %copy-start = (bf16[1,32,2,128,128]{4,3,2,1,0:T(8,128)(2,1)S(1)}, bf16[1,32,2,128,128]{4,3,2,1,0:T(8,128)(2,1)}, u32[]{:S(2)}) copy-start(bf16[1,32,2,128,128]{4,3,2,1,0:T(8,128)(2,1)} %param.12) | copy-start | bytes 6291460
  6.5 58.7 %all-gather.2.cloned.1.call-start = ((), (), s32[]{:S(2)}) async-start(), calls=%async_computation.2 | async-start | bytes 4718592 | tf_op jit(solution)/shard_map/all_gather | solution.py:12
  8.6 77.9 %all-to-all-start = ((s32[32,1,2]{2,1,0:T(1,128)}), s32[32,1,2]{2,1,0:T(1,128)S(1)}, u32[]{:S(2)}, u32[]{:S(2)}) async-start(s32[32,1,2]{2,1,0:T(1,128)} %copy.29), calls=%async_computation | async-start | bytes 32768 | tf_op jit(solution)/shard_map/all_to_all | solution.py:25
  75.7 10.4 %copy-start.2 = (bf16[512,512]{1,0:T(8,128)(2,1)S(1)}, bf16[512,512]{1,0:T(8,128)(2,1)}, u32[]{:S(2)}) copy-start(bf16[512,512]{1,0:T(8,128)(2,1)} %param.8) | copy-start | bytes 1572868
  92.5 220.5 %all-to-all-start.1 = ((bf16[32,512,512]{2,1,0:T(8,128)(2,1)}), bf16[32,512,512]{2,1,0:T(8,128)(2,1)}, u32[]{:S(2)}, u32[]{:S(2)}) async-start(bf16[32,512,512]{2,1,0:T(8,128)(2,1)} %stack.2), calls=%async_computation.1 | async-start | bytes 33554432 | tf_op jit(solution)/shard_map/all_to_all | solution.py:27
  348.0 20.0 %copy-start.1 = (s32[1,32,2]{1,2,0:T(2,128)S(1)}, s32[1,32,2]{1,2,0:T(2,128)}, u32[]{:S(2)}) copy-start(s32[1,32,2]{1,2,0:T(2,128)} %param.13) | copy-start | bytes 772
Sparse Core Ops, SparseCore 0:
  9.1 56.0 all-gather.1
